TPU v7x, 32 devices: a whole 2x2x4 slice. The times are simulated.
32 devices in a mesh: row: 8 (over y, x, core), col: 4 (over z).
Axes of the slice: x: 2, y: 2, z: 4, core: 2. Of those that a mesh axis runs over, the one named last changes fastest.
Arguments:
- covariance: float32 [4096, 2, 2048], P('row', None, 'col'), may hold values from 0 to 1.1, as said below
- diag_inverse: float32 [512, 512], replicated, as said below
Outputs:
- panels: float32 [4096, 1024], P('row', 'col')
- trailing: float32 [4096, 2, 2048], P('row', None, 'col')
Inputs may be any that keep to these rules, and one draw needn't show every extreme that they name: `covariance`: K is symmetric and positive definite, its smallest eigenvalue 0.1 or more. `diag_inverse`: the inverse of the lower Cholesky factor of K[0:512, 0:512].
All inputs are finite; a program needn't handle non-finite values.
Results may differ from a plain program's by a relative error of at most 0.0003.
Values sent between devices are 32-bit elements; how exact they have to be, the bound alone decides.
No kernel may reach another device: no remote copies, remote signals or barrier semaphores. Data moves between devices by JAX's collectives and lax.ppermute only.
A program may use at most 128 MiB of HBM per device.

v0:
```python
import jax
import jax.numpy as jnp
from jax import lax
from jax.sharding import PartitionSpec as P

highest = lax.Precision.HIGHEST


def broadcast(array, axis, root):
    mine = lax.axis_index(axis) == root
    return lax.psum(jnp.where(mine, array, jnp.zeros_like(array)), axis)


def outer_product(left, right):
    return lax.dot_general(
        left, right, (((1,), (1,)), ((), ())), precision=highest, preferred_element_type=jnp.float32
    )


def local(covariance, diag_inverse):
    tile_size = covariance.shape[0]
    row_index = lax.axis_index("row")
    col_index = lax.axis_index("col")
    col_count = lax.axis_size("col")
    cycles = lax.axis_size("row") // col_count
    columns = [position * col_count + col_index for position in range(cycles)]
    block_tiles = [covariance[:, position, :] for position in range(cycles)]
    zero_tile = jnp.zeros((tile_size, tile_size), jnp.float32)
    local_first = lax.cond(
        col_index == 0, lambda: outer_product(block_tiles[0], diag_inverse), lambda: zero_tile
    )
    own_first = broadcast(local_first, "col", 0)
    slot_tiles = jnp.stack([jnp.where(row_index == column, own_first, 0.0) for column in columns])
    summed_first = lax.psum(slot_tiles, "row")
    remote_first = [summed_first[position] for position in range(cycles)]

    def lower_update(current, own_panel, remote_panel, column, first_col):
        keep_mask = (row_index >= column) & (column >= first_col)
        return lax.cond(
            keep_mask, lambda: current - outer_product(own_panel, remote_panel), lambda: current
        )

    block_tiles = [
        lower_update(block_tiles[position], own_first, remote_first[position], columns[position], 1)
        for position in range(cycles)
    ]
    is_owner = (row_index == 1) & (col_index == 1)
    identity = jnp.eye(tile_size, dtype=jnp.float32)
    factor_local = jnp.linalg.cholesky(jnp.where(is_owner, block_tiles[0], identity))
    factor = broadcast(factor_local, "row", 1)

    def solve_panel():
        solved = jax.scipy.linalg.solve_triangular(factor, block_tiles[0].T, lower=True).T
        return jnp.where(row_index >= 1, solved, 0.0)

    local_second = lax.cond(col_index == 1, solve_panel, lambda: zero_tile)
    own_second = broadcast(local_second, "col", 1)
    slot_second = jnp.stack([jnp.where(row_index == column, own_second, 0.0) for column in columns])
    summed_second = lax.psum(slot_second, "row")
    remote_second = [summed_second[position] for position in range(cycles)]
    block_tiles = [
        lower_update(
            block_tiles[position], own_second, remote_second[position], columns[position], 2
        )
        for position in range(cycles)
    ]
    finals = [
        jnp.where(
            (row_index >= columns[position]) & (columns[position] >= 2), block_tiles[position], 0.0
        )
        for position in range(cycles)
    ]
    trailing = jnp.stack(finals, axis=1)
    both_panels = jnp.concatenate([own_first, own_second], axis=1)
    share_width = both_panels.shape[1] // col_count
    panels = lax.dynamic_slice_in_dim(both_panels, col_index * share_width, share_width, 1)
    return (panels, trailing)


def solution(mesh):
    return jax.shard_map(
        local,
        mesh=mesh,
        in_specs=(P("row", None, "col"), P()),
        out_specs=(P("row", "col"), P("row", None, "col")),
        check_vma=False,
    )
```

profile of v0, /device:TPU:22, one launch (start us, length us, event | category | flops | bytes accessed | tf_op | source)
XLA Modules:
  0.0 480.6 jit_solution(18360229636380562185)
XLA Ops:
  7.2 5.0 %fusion.42 = (f32[512,1,512]{2,1,0:T(1,128)}, f32[512,1,512]{2,1,0:T(1,128)S(1)}) fusion(f32[512,2,512]{2,1,0:T(2,128)} %param.14), kind=kLoop, calls=%fused_computation.100 | loop fusion | bytes 4194304 | tf_op jit(solution)/shard_map/slice | solution.py:27
  14.7 52.3 %all-reduce.7.cloned.1.call-done = f32[512,512]{1,0:T(8,128)} async-done(((f32[512,512]{1,0:T(8,128)}), f32[512,512]{1,0:T(8,128)}) %all-reduce.7.cloned.1.call-update) | async-done | bytes 1048592 | tf_op jit(solution)/shard_map/psum | solution.py:11
  67.0 1.4 select_bitcast_fusion.5
  68.4 1.5 pad_maximum_fusion
  70.0 60.8 %all-reduce.9.cloned.1.call-done = f32[2,512,512]{2,1,0:T(8,128)} async-done(((f32[2,512,512]{2,1,0:T(8,128)}), f32[2,512,512]{2,1,0:T(8,128)}) %all-reduce.9.cloned.1.call-update) | async-done | bytes 2097168 | tf_op jit(solution)/shard_map/psum | solution.py:34
  130.8 3.9 conditional.7
  130.8 3.4 convolution_subtract_fusion
  136.1 2.5 copy.7
  138.7 1.5 fusion.28
  141.1 11.7 %cholesky.103 = f32[128,128]{1,0:T(8,128)S(1)} custom-call(f32[128,128]{1,0:T(8,128)S(1)} %cholesky.263), custom_call_target="Cholesky" | custom-call | tf_op jit(solution)/shard_map/jit(cholesky)/cholesky | solution.py:49
  152.9 9.8 %custom-call.31 = f32[1,128,128]{1,2,0:T(8,128)S(1)} custom-call(f32[1,128,128]{2,1,0:T(8,128)S(1)} %get-tuple-element.121), custom_call_target="InvertDiagBlocksLowerTriangular" | custom-call | tf_op jit(solution)/shard_map/jit(cholesky)/cholesky | solution.py:49
  162.8 1.2 constant_dynamic-update-slice_fusion.1
  164.0 1.3 convolution_subtract_fusion.7
  165.3 11.7 %cholesky.215 = f32[128,128]{1,0:T(8,128)S(1)} custom-call(f32[128,128]{1,0:T(8,128)S(1)} %cholesky.267), custom_call_target="Cholesky" | custom-call | tf_op jit(solution)/shard_map/jit(cholesky)/cholesky | solution.py:49
  177.1 10.0 %custom-call.32 = f32[1,128,128]{1,2,0:T(8,128)S(1)} custom-call(f32[1,128,128]{2,1,0:T(8,128)S(1)} %get-tuple-element.118), custom_call_target="InvertDiagBlocksLowerTriangular" | custom-call | tf_op jit(solution)/shard_map/jit(cholesky)/cholesky | solution.py:49
  187.3 1.3 convolution_subtract_fusion.8
  188.6 11.7 %cholesky.236 = f32[128,128]{1,0:T(8,128)S(1)} custom-call(f32[128,128]{1,0:T(8,128)S(1)} %cholesky.272), custom_call_target="Cholesky" | custom-call | tf_op jit(solution)/shard_map/jit(cholesky)/cholesky | solution.py:49
  201.0 9.8 %custom-call.33 = f32[1,128,128]{1,2,0:T(8,128)S(1)} custom-call(f32[1,128,128]{2,1,0:T(8,128)S(1)} %get-tuple-element.115), custom_call_target="InvertDiagBlocksLowerTriangular" | custom-call | tf_op jit(solution)/shard_map/jit(cholesky)/cholesky | solution.py:49
  212.3 11.9 %cholesky.253 = f32[128,128]{1,0:T(8,128)S(1)} custom-call(f32[128,128]{1,0:T(8,128)S(1)} %convolution_subtract_fusion.9), custom_call_target="Cholesky" | custom-call | tf_op jit(solution)/shard_map/jit(cholesky)/cholesky | solution.py:49
  229.3 56.1 %all-reduce.11.cloned.1.call-done = f32[512,512]{1,0:T(8,128)} async-done(((f32[512,512]{1,0:T(8,128)}), f32[512,512]{1,0:T(8,128)}) %all-reduce.11.cloned.1.call-update) | async-done | bytes 1048592 | tf_op jit(solution)/shard_map/psum | solution.py:11
  287.6 108.0 %all-reduce.13.cloned.1.call-done = f32[512,512]{1,0:T(8,128)} async-done(((f32[512,512]{1,0:T(8,128)}), f32[512,512]{1,0:T(8,128)}) %all-reduce.13.cloned.1.call-update) | async-done | bytes 1048592 | tf_op jit(solution)/shard_map/psum | solution.py:11
  395.6 1.5 select_bitcast_fusion.3
  397.0 1.5 pad_maximum_fusion.1
  400.8 4.5 conditional.10
  400.8 4.5 convolution_subtract_fusion.2
  406.2 53.0 %all-reduce.15.cloned.1.call-done = f32[2,512,512]{2,1,0:T(8,128)} async-done(((f32[2,512,512]{2,1,0:T(8,128)}), f32[2,512,512]{2,1,0:T(8,128)}) %all-reduce.15.cloned.1.call-update) | async-done | bytes 2097168 | tf_op jit(solution)/shard_map/psum | solution.py:59
  459.2 4.6 conditional.11
  459.4 4.4 convolution_subtract_fusion.3
  463.8 2.3 select_bitcast_fusion
  466.1 3.4 conditional.9
  466.1 3.4 convolution_subtract_fusion.1
  470.9 2.9 copy.10
  (50 shorter events, 18.1 us)
Async XLA Ops:
  7.2 59.8 %all-reduce.7.cloned.1.call-start = ((), (), s32[]{:S(2)}) async-start(), calls=%async_computation | async-start | bytes 2097152 | tf_op jit(solution)/shard_map/psum | solution.py:11
  12.2 1.2 copy-start.5
  14.7 116.1 %all-reduce.9.cloned.1.call-start = ((), (), s32[]{:S(2)}) async-start(), calls=%async_computation.1 | async-start | bytes 4194304 | tf_op jit(solution)/shard_map/psum | solution.py:34
  69.9 60.9 %copy-start = (f32[512,512]{1,0:T(8,128)S(1)}, f32[512,512]{1,0:T(8,128)}, u32[]{:S(2)}) copy-start(f32[512,512]{1,0:T(8,128)} %all-reduce.7.cloned.1.call-done) | copy-start | bytes 3145732
  69.9 215.4 %all-reduce.11.cloned.1.call-start = ((), (), s32[]{:S(2)}) async-start(), calls=%async_computation.2 | async-start | bytes 2097152 | tf_op jit(solution)/shard_map/psum | solution.py:11
  140.1 1.0 copy-start.4
  229.2 166.3 %all-reduce.13.cloned.1.call-start = ((), (), s32[]{:S(2)}) async-start(), calls=%async_computation.3 | async-start | bytes 2097152 | tf_op jit(solution)/shard_map/psum | solution.py:11
  287.5 171.6 %all-reduce.15.cloned.1.call-start = ((), (), s32[]{:S(2)}) async-start(), calls=%async_computation.4 | async-start | bytes 4194304 | tf_op jit(solution)/shard_map/psum | solution.py:59
  398.5 1.2 copy-start.3
  400.8 4.5 copy-start.1
  469.4 1.2 copy-start.2
Sparse Core Ops, SparseCore 0:
  14.8 52.1 all-reduce.6
  70.8 59.9 all-reduce.8
  229.4 55.9 all-reduce.10
  288.1 107.3 all-reduce.12
  399.2 59.9 all-reduce.14
where the time goes:
time: 487 us; the launch traced here: 481 us
  waiting for transfers between devices  330 us (68%)
  other arithmetic  93.9 us (19%)
  matrix products  21 us (4%)
  local copies, waits for them, and re-layouts  17.7 us (4%)
  between operations  16.8 us (3%)
    psum x3, waiting for transfers between devices, broadcast(): return lax.psum(jnp.where(mine, array, jnp.zeros_like(array)), axis)  216 us
    another operation x14, other arithmetic, local(): jnp.linalg.cholesky(jnp.where(is_owner, block_tiles[0], identity))  78.8 us
    psum x1, waiting for transfers between devices, local(): summed_first = lax.psum(slot_tiles, 'row')  60.8 us
    psum x1, waiting for transfers between devices, local(): summed_second = lax.psum(slot_second, 'row')  53 us
    dot_general x4, matrix products, outer_product(): lax.dot_general(left, right, (((1,), (1,)), ((), ())), precision=highest,...  15.6 us
  transfers between devices with their start and end apart: 5, of which 5 were waited for; matrix products, arithmetic and copies ran while one was open for 1% of the time, Pallas kernels for 0%

commit v1 on v0

--- a/solution.py
+++ b/solution.py
@@ -8,7 +8,7 @@
 
 def broadcast(array, axis, root):
     mine = lax.axis_index(axis) == root
-    return lax.psum(jnp.where(mine, array, jnp.zeros_like(array)), axis)
+    return jnp.sum(lax.all_gather(jnp.where(mine, array, jnp.zeros_like(array)), axis), axis=0)
 
 
 def outer_product(left, right):

time: 487 us -> 551 us (1.13)
  waiting for transfers between devices: 330 us -> 387 us
  other arithmetic: 93.9 us -> 102 us
    all_gather x0 -> x3, waiting for transfers between devices: none -> 274 us  [broadcast(): lax.all_gather(jnp.where(mine, array, jnp.zeros_like(array)), axis)]
    psum x3 -> x0, waiting for transfers between devices: 216 us -> none  [broadcast(): return lax.psum(jnp.where(mine, array, jnp.zeros_like(array)), axis)]
    reduce_sum x0 -> x3, other arithmetic: none -> 10 us  [broadcast(): jnp.sum(lax.all_gather(jnp.where(mine, array, jnp.zeros_like(array)), axi...]
where the time goes in v1:
time: 551 us; the launch traced here: 544 us
  waiting for transfers between devices  387 us (70%)
  other arithmetic  102 us (19%)
  matrix products  21 us (4%)
  local copies, waits for them, and re-layouts  17.8 us (3%)
  between operations  16.8 us (3%)
    all_gather x3, waiting for transfers between devices, broadcast(): lax.all_gather(jnp.where(mine, array, jnp.zeros_like(array)), axis)  274 us
    another operation x14, other arithmetic, local(): jnp.linalg.cholesky(jnp.where(is_owner, block_tiles[0], identity))  79 us
    psum x1, waiting for transfers between devices, local(): summed_first = lax.psum(slot_tiles, 'row')  60 us
    psum x1, waiting for transfers between devices, local(): summed_second = lax.psum(slot_second, 'row')  52.3 us
    dot_general x4, matrix products, outer_product(): lax.dot_general(left, right, (((1,), (1,)), ((), ())), precision=highest,...  15.5 us
  transfers between devices with their start and end apart: 5, of which 5 were waited for; matrix products, arithmetic and copies ran while one was open for 1% of the time, Pallas kernels for 0%

profile of v1, /device:TPU:22, one launch (start us, length us, event | category | flops | bytes accessed | tf_op | source)
XLA Modules:
  0.0 544.4 jit_solution(1303182649543489633)
XLA Ops:
  7.2 5.0 fusion.42
  14.7 80.3 %all-gather.7.cloned.1.call-done = f32[2048,512]{1,0:T(8,128)} async-done(((f32[512,512]{1,0:T(8,128)}), f32[2048,512]{1,0:T(8,128)}) %all-gather.7.cloned.1.call-update) | async-done | bytes 4194320 | tf_op jit(solution)/shard_map/all_gather | solution.py:11
  95.0 2.8 reduce_sum.27
  98.1 1.5 pad_maximum_fusion
  99.7 60.0 %all-reduce.4.cloned.1.call-done = f32[2,512,512]{2,1,0:T(8,128)} async-done(((f32[2,512,512]{2,1,0:T(8,128)}), f32[2,512,512]{2,1,0:T(8,128)}) %all-reduce.4.cloned.1.call-update) | async-done | bytes 2097168 | tf_op jit(solution)/shard_map/psum | solution.py:34
  159.7 3.5 conditional.7
  159.7 3.4 convolution_subtract_fusion
  164.7 2.5 copy.7
  167.2 1.5 fusion.28
  169.6 11.7 %cholesky.103 = f32[128,128]{1,0:T(8,128)S(1)} custom-call(f32[128,128]{1,0:T(8,128)S(1)} %cholesky.263), custom_call_target="Cholesky" | custom-call | tf_op jit(solution)/shard_map/jit(cholesky)/cholesky | solution.py:49
  181.5 9.8 %custom-call.31 = f32[1,128,128]{1,2,0:T(8,128)S(1)} custom-call(f32[1,128,128]{2,1,0:T(8,128)S(1)} %get-tuple-element.121), custom_call_target="InvertDiagBlocksLowerTriangular" | custom-call | tf_op jit(solution)/shard_map/jit(cholesky)/cholesky | solution.py:49
  193.9 11.7 %cholesky.215 = f32[128,128]{1,0:T(8,128)S(1)} custom-call(f32[128,128]{1,0:T(8,128)S(1)} %cholesky.267), custom_call_target="Cholesky" | custom-call | tf_op jit(solution)/shard_map/jit(cholesky)/cholesky | solution.py:49
  205.6 10.0 %custom-call.32 = f32[1,128,128]{1,2,0:T(8,128)S(1)} custom-call(f32[1,128,128]{2,1,0:T(8,128)S(1)} %get-tuple-element.118), custom_call_target="InvertDiagBlocksLowerTriangular" | custom-call | tf_op jit(solution)/shard_map/jit(cholesky)/cholesky | solution.py:49
  215.9 1.3 convolution_subtract_fusion.8
  217.2 11.7 %cholesky.236 = f32[128,128]{1,0:T(8,128)S(1)} custom-call(f32[128,128]{1,0:T(8,128)S(1)} %cholesky.272), custom_call_target="Cholesky" | custom-call | tf_op jit(solution)/shard_map/jit(cholesky)/cholesky | solution.py:49
  229.6 9.8 %custom-call.33 = f32[1,128,128]{1,2,0:T(8,128)S(1)} custom-call(f32[1,128,128]{2,1,0:T(8,128)S(1)} %get-tuple-element.115), custom_call_target="InvertDiagBlocksLowerTriangular" | custom-call | tf_op jit(solution)/shard_map/jit(cholesky)/cholesky | solution.py:49
  240.9 12.1 %cholesky.253 = f32[128,128]{1,0:T(8,128)S(1)} custom-call(f32[128,128]{1,0:T(8,128)S(1)} %convolution_subtract_fusion.9), custom_call_target="Cholesky" | custom-call | tf_op jit(solution)/shard_map/jit(cholesky)/cholesky | solution.py:49
  258.1 54.3 %all-gather.9.cloned.1.call-done = f32[4096,512]{1,0:T(8,128)} async-done(((f32[512,512]{1,0:T(8,128)}), f32[4096,512]{1,0:T(8,128)}) %all-gather.9.cloned.1.call-update) | async-done | bytes 8388624 | tf_op jit(solution)/shard_map/all_gather | solution.py:11
  312.4 4.5 reduce_sum.28
  319.2 139.5 %all-gather.11.cloned.1.call-done = f32[2048,512]{1,0:T(8,128)} async-done(((f32[512,512]{1,0:T(8,128)}), f32[2048,512]{1,0:T(8,128)}) %all-gather.11.cloned.1.call-update) | async-done | bytes 4194320 | tf_op jit(solution)/shard_map/all_gather | solution.py:11
  458.6 2.8 reduce_sum.29
  461.7 1.5 pad_maximum_fusion.1
  463.2 2.3 copy.17
  465.5 4.5 conditional.10
  465.5 4.4 convolution_subtract_fusion.2
  471.0 52.3 %all-reduce.6.cloned.1.call-done = f32[2,512,512]{2,1,0:T(8,128)} async-done(((f32[2,512,512]{2,1,0:T(8,128)}), f32[2,512,512]{2,1,0:T(8,128)}) %all-reduce.6.cloned.1.call-update) | async-done | bytes 2097168 | tf_op jit(solution)/shard_map/psum | solution.py:59
  523.3 4.4 conditional.11
  523.3 4.4 convolution_subtract_fusion.3
  527.7 2.3 select_bitcast_fusion
  530.0 3.4 conditional.9
  530.0 3.4 convolution_subtract_fusion.1
  534.8 2.9 copy.10
  (47 shorter events, 19.0 us)
Async XLA Ops:
  7.2 87.9 %all-gather.7.cloned.1.call-start = ((), (), s32[]{:S(2)}) async-start(), calls=%async_computation.2 | async-start | bytes 5242880 | tf_op jit(solution)/shard_map/all_gather | solution.py:11
  12.2 1.2 copy-start.2
  14.7 145.0 %all-reduce.4.cloned.1.call-start = ((), (), s32[]{:S(2)}) async-start(), calls=%async_computation | async-start | bytes 4194304 | tf_op jit(solution)/shard_map/psum | solution.py:34
  99.6 212.8 %all-gather.9.cloned.1.call-start = ((), (), s32[]{:S(2)}) async-start(), calls=%async_computation.3 | async-start | bytes 9437184 | tf_op jit(solution)/shard_map/all_gather | solution.py:11
  168.7 1.0 copy-start.1
  258.0 200.6 %all-gather.11.cloned.1.call-start = ((), (), s32[]{:S(2)}) async-start(), calls=%async_computation.4 | async-start | bytes 5242880 | tf_op jit(solution)/shard_map/all_gather | solution.py:11
  319.1 204.2 %all-reduce.6.cloned.1.call-start = ((), (), s32[]{:S(2)}) async-start(), calls=%async_computation.1 | async-start | bytes 4194304 | tf_op jit(solution)/shard_map/psum | solution.py:59
  533.3 1.2 copy-start
Sparse Core Ops, SparseCore 0:
  14.8 80.2 all-gather.6
  99.7 59.8 all-reduce.3
  258.1 54.2 all-gather.8
  319.2 139.3 all-gather.10
  463.3 59.8 all-reduce.5
